TPU v7x, 512 devices: a whole 4x4x16 slice. The times are simulated.
512 devices in a mesh: prow: 16 (over y_hi, x, core), pcol: 32 (over y_lo, z).
Axes of the slice: x: 4, y: 4 (y_hi: 2, y_lo: 2; y = y_hi * 2 + y_lo), z: 16, core: 2. Of those that a mesh axis runs over, the one named last changes fastest.
Arguments:
- sep_inverse: bfloat16 [2, 16, 256, 1, 32, 256], P(None, 'prow', None, None, 'pcol'), may hold values from -2 to 30, as said below
- panels: bfloat16 [4, 2, 16, 256, 256], P(None, None, 'prow', 'pcol'), may hold values from -0.0625 to 0.0625
- ancestors: int32 [4, 32], replicated, may hold values from 0 to 1, as said below
- window_factor: bfloat16 [6, 256, 256], replicated, may hold values from -0.1875 to 0.1875
- diag_inverse: bfloat16 [4, 256, 256], replicated, may hold values from -1 to 4, as said below
Outputs:
- ys: float32 [4, 2, 16, 256, 256], P(None, None, 'prow', 'pcol')
- window_inverse: float32 [1024, 1024], P('prow', 'pcol')
Inputs may be any that keep to these rules, and one draw needn't show every extreme that they name: sep_inverse read as in the first step is symmetric. `diag_inverse`: each block is symmetric. ancestors[k + 1, t] <= ancestors[k, t]: a supernode's ancestor tiles lie among those of the one before it.
All inputs are finite; a program needn't handle non-finite values.
Results may differ from a plain program's by a relative error of at most 0.00035.
Values may be sent and summed in bfloat16 or wider, within the bound.
A program may use at most 64 MiB of HBM per device.

v0:
```python
import jax
import jax.numpy as jnp
from jax import lax
from jax.sharding import PartitionSpec as P


def broadcast(block, axis, owner):
    block = jnp.where(lax.axis_index(axis) == owner, block, jnp.zeros_like(block))
    return lax.psum(block, axis)


def product(operand_left, operand_right):
    return jnp.dot(
        operand_left,
        operand_right,
        precision=lax.Precision.HIGHEST,
        preferred_element_type=jnp.float32,
    )


def pair_index(earlier, later):
    return later * (later - 1) // 2 + earlier


def window_step(later, window_sums, window_factor, diag_inverse, window_blocks):
    coupled = []
    for earlier in range(later):
        running = window_sums[earlier]
        for partner in range(later):
            running = running + product(
                window_blocks[earlier, partner],
                window_factor[pair_index(partner, later)].astype(jnp.float32),
            )
        upper_block = -running
        window_blocks[earlier, later] = upper_block
        window_blocks[later, earlier] = upper_block.T
        coupled.append(upper_block)
    running = window_sums[later]
    for earlier in range(later):
        running = running + product(
            window_factor[pair_index(earlier, later)].astype(jnp.float32).T, coupled[earlier]
        )
    window_blocks[later, later] = diag_inverse[later].astype(jnp.float32) - running


def assemble_window(window_blocks, supernodes):
    return jnp.block(
        [
            [window_blocks[first, second] for second in range(supernodes)]
            for first in range(supernodes)
        ]
    )


def per_device(sep_inverse, panels, ancestors, window_factor, diag_inverse):
    prow_count = lax.axis_size("prow")
    pcol_count = lax.axis_size("pcol")
    row_index = lax.axis_index("prow")
    column_index = lax.axis_index("pcol")
    tile_rows = sep_inverse.shape[0]
    width = sep_inverse.shape[2]
    owned_count = sep_inverse.shape[3]
    supernodes = panels.shape[0]
    slice_rows = panels.shape[3]
    group_ratio = pcol_count // prow_count
    local_sep = sep_inverse.reshape(tile_rows, width, owned_count, width)
    window_blocks = {}
    columns = []
    for later in range(supernodes):
        tile_flags = lax.dynamic_slice_in_dim(
            ancestors[later].reshape(tile_rows, prow_count), row_index, 1, 1
        )
        keep_tiles = tile_flags.astype(jnp.bfloat16).reshape(tile_rows, 1, 1)
        own_piece = panels[later, :, 0] * keep_tiles
        full_rows = lax.all_gather(own_piece, "pcol", axis=1, tiled=True)
        grouped = full_rows.reshape(owned_count, group_ratio, width, width)
        picked = lax.dynamic_slice_in_dim(grouped, column_index // prow_count, 1, 1)[:, 0]
        owned_tiles = broadcast(picked, "prow", column_index % prow_count)

        def row_term(first_row, row_count, owned_tiles=owned_tiles):
            return jnp.einsum(
                "rbcd,cde->bre", local_sep, owned_tiles, preferred_element_type=jnp.float32
            )

        summed = lax.psum_scatter(
            row_term(jnp.int32(0), slice_rows * lax.axis_size("pcol")),
            "pcol",
            scatter_dimension=0,
            tiled=True,
        )
        row_total = jnp.transpose(summed, (1, 0, 2)).reshape(tile_rows * slice_rows, width)
        row_keep = jnp.repeat(
            tile_flags[:, 0].astype(jnp.float32),
            slice_rows,
            total_repeat_length=tile_rows * slice_rows,
        )
        carried = -row_total
        for earlier in range(later):
            carried = carried - product(
                columns[earlier], window_factor[pair_index(earlier, later)].astype(jnp.float32)
            )
        current = carried * row_keep[:, None]
        factor_rows = own_piece.reshape(tile_rows * slice_rows, width).astype(jnp.float32)
        window_parts = [product(columns[earlier].T, factor_rows) for earlier in range(later)]
        window_parts.append(product(factor_rows.T, current))
        window_sums = lax.psum(jnp.stack(window_parts), ("prow", "pcol"))
        window_step(later, window_sums, window_factor, diag_inverse, window_blocks)
        columns.append(current)
    ys = jnp.stack(columns).reshape(supernodes, tile_rows, 1, slice_rows, width)
    whole_window = assemble_window(window_blocks, supernodes)
    rows_each = supernodes * width // prow_count
    cols_each = supernodes * width // pcol_count
    local_window = lax.dynamic_slice(
        whole_window, (row_index * rows_each, column_index * cols_each), (rows_each, cols_each)
    )
    return (ys, local_window)


def solution(mesh):
    placed = (
        P(None, "prow", None, None, "pcol", None),
        P(None, None, "prow", "pcol", None),
        P(),
        P(),
        P(),
    )
    return jax.shard_map(
        per_device,
        mesh=mesh,
        in_specs=placed,
        out_specs=(P(None, None, "prow", "pcol", None), P("prow", "pcol")),
        check_vma=False,
    )
```

profile of v0, /device:TPU:4, one launch (start us, length us, event | category | flops | bytes accessed | tf_op | source)
XLA Modules:
  0.0 1206.1 jit_solution(4849116906709062268)
XLA Ops:
  7.3 0.8 slice_reduce_fusion.1
  8.9 0.8 bitcast_multiply_fusion.6
  9.8 70.2 %all_gather.12 = bf16[2,256,256]{2,0,1:T(2,128)(2,1)S(1)} all-gather(bf16[2,8,256]{2,0,1:T(2,128)(2,1)S(1)} %copy.58), channel_id=1, replica_groups=mesh['prow'=16,'pcol'=32] {'pcol'}, dimensions={1}, use_global_device_ids=true | all-gather | bytes 270336 | tf_op jit(solution)/shard_map/all_gather | solution.py:75
  80.4 59.8 %all_gather.13 = bf16[2,256,256]{2,0,1:T(2,128)(2,1)S(1)} all-gather(bf16[2,8,256]{2,0,1:T(2,128)(2,1)S(1)} %copy.63), channel_id=1, replica_groups=mesh['prow'=16,'pcol'=32] {'pcol'}, dimensions={1}, use_global_device_ids=true | all-gather | bytes 270336 | tf_op jit(solution)/shard_map/all_gather | solution.py:75
  140.7 0.7 select_bitcast_fusion.3
  141.3 0.6 select_bitcast_fusion.2
  142.0 61.7 %all_gather.15 = bf16[2,256,256]{2,0,1:T(2,128)(2,1)S(1)} all-gather(bf16[2,8,256]{2,0,1:T(2,128)(2,1)S(1)} %copy.73), channel_id=1, replica_groups=mesh['prow'=16,'pcol'=32] {'pcol'}, dimensions={1}, use_global_device_ids=true | all-gather | bytes 270336 | tf_op jit(solution)/shard_map/all_gather | solution.py:75
  204.1 0.7 select_bitcast_fusion
  204.8 59.8 %all_gather.14 = bf16[2,256,256]{2,0,1:T(2,128)(2,1)S(1)} all-gather(bf16[2,8,256]{2,0,1:T(2,128)(2,1)S(1)} %copy.68), channel_id=1, replica_groups=mesh['prow'=16,'pcol'=32] {'pcol'}, dimensions={1}, use_global_device_ids=true | all-gather | bytes 270336 | tf_op jit(solution)/shard_map/all_gather | solution.py:75
  265.0 0.7 select_bitcast_fusion.1
  265.8 141.1 %all-reduce.15.cloned.1.call-done = (bf16[256,256]{0,1:T(8,128)(2,1)}, bf16[256,256]{0,1:T(8,128)(2,1)}, bf16[256,256]{0,1:T(8,128)(2,1)}, bf16[256,256]{0,1:T(8,128)(2,1)}) async-done(((bf16[256,256]{0,1:T(8,128)(2,1)}, bf16[256,256]{0,1:T(8,128)(2,1)}, bf16[256,256]{0,1:T(8,128)(2,1)}, bf16[256,256]{0,1:T(8,128)(2,1)}), (bf16[256,256]{0,1:T(8,128)(2,1)}, bf16[256,256]{0,1:T(8,128)(2,1)}, ...) | async-done | bytes 524304 | tf_op jit(solution)/shard_map/psum | solution.py:9
  406.9 1.2 convolution_bitcast_fusion
  408.1 1.0 copy.75
  409.3 1.0 copy.60
  410.6 1.0 copy.65
  411.9 1.0 copy.70
  414.1 0.6 fusion.134
  414.7 0.6 fusion.135
  415.3 0.7 fusion.136
  415.9 0.6 fusion.137
  416.5 5.0 broadcast_select_fusion
  421.6 1.3 dynamic-slice.31
  423.5 262.1 %all-reduce.13.cloned.1.call-done = (f32[256,2,256]{2,1,0:T(2,128)}, f32[256,2,256]{2,1,0:T(2,128)}, f32[256,2,256]{2,1,0:T(2,128)}, f32[256,2,256]{2,1,0:T(2,128)}) async-done(((f32[256,2,256]{2,1,0:T(2,128)}, f32[256,2,256]{2,1,0:T(2,128)}, f32[256,2,256]{2,1,0:T(2,128)}, f32[256,2,256]{2,1,0:T(2,128)}), (f32[256,2,256]{2,1,0:T(2,128)}, f32[256,2,256]{2,1,0:T(2,128)}, f32[256,2,256]{2,1,0:T(2,128)}, ...) | async-done | bytes 2097168
  685.7 0.7 constant_dynamic-slice_fusion.11
  686.4 0.4 convolution_bitcast_fusion.13
  686.8 0.4 convolution_bitcast_fusion.16
  687.2 0.4 convolution_bitcast_fusion.18
  687.6 1.1 convolution_bitcast_fusion.19
  688.7 0.7 constant_dynamic-slice_fusion.10
  689.4 0.7 constant_dynamic-slice_fusion.9
  690.5 0.3 convolution_bitcast_fusion.15
  691.0 0.4 convolution_bitcast_fusion.14
  691.5 0.3 convolution_bitcast_fusion.11
  691.8 0.3 convolution_bitcast_fusion.12
  692.1 0.7 constant_dynamic-slice_fusion.8
  693.2 0.4 convolution_bitcast_fusion.17
  693.8 0.4 convolution_bitcast_fusion.10
  694.2 0.8 pad_maximum_fusion.2
  695.0 0.9 pad_maximum_fusion.1
  696.0 1.1 pad_maximum_fusion
  697.2 0.6 pad_maximum_fusion.3
  697.8 481.1 %all-reduce.11.cloned.1.call-done = (f32[1,256,256]{2,1,0:T(8,128)}, f32[4,256,256]{2,1,0:T(8,128)}, f32[2,256,256]{2,1,0:T(8,128)}, f32[3,256,256]{2,1,0:T(8,128)}) async-done(((f32[1,256,256]{2,1,0:T(8,128)}, f32[4,256,256]{2,1,0:T(8,128)}, f32[2,256,256]{2,1,0:T(8,128)}, f32[3,256,256]{2,1,0:T(8,128)}), (f32[1,256,256]{2,1,0:T(8,128)}, f32[4,256,256]{2,1,0:T(8,128)}, f32[2,256,256]{2,1,0:T(8,128)}, ...) | async-done | bytes 2621456 | tf_op jit(solution)/shard_map/psum | solution.py:106
  1178.9 1.0 subtract_bitcast_fusion
  1179.9 1.3 fusion.14
  1181.2 0.3 fusion.11
  1181.6 0.4 convolution_add_fusion.5
  1182.2 0.4 copy-done.5
  1182.7 0.4 convolution_add_fusion.7
  1183.6 1.0 fusion.7
  1184.7 0.4 convolution_add_fusion.2
  1185.1 0.8 copy.82
  1186.7 0.9 copy.86
  1187.6 0.9 copy.91
  1189.0 0.4 copy-done.4
  1189.4 1.2 fusion.6
  1190.6 0.8 copy.85
  1191.4 2.0 fusion.3
  1193.4 0.8 copy.90
  1194.3 0.4 convolution_add_fusion.1
  1194.7 0.6 copy-done.3
  1195.2 0.3 fusion.2
  1195.8 1.9 fusion.1
  1197.9 1.1 maximum_maximum_fusion
  1198.9 0.7 copy.93
  (76 shorter events, 8.4 us)
Async XLA Ops:
  7.2 399.7 %copy-start = (bf16[2,1,256,1,1,256]{5,2,4,3,1,0:T(8,128)(2,1)S(1)}, bf16[2,1,256,1,1,256]{5,2,4,3,1,0:T(8,128)(2,1)}, u32[]{:S(2)}) copy-start(bf16[2,1,256,1,1,256]{5,2,4,3,1,0:T(8,128)(2,1)} %param.15) | copy-start | bytes 786436
  7.2 399.7 %all-reduce.15.cloned.1.call-start = ((), (), s32[]{:S(2)}) async-start(), calls=%async_computation.2 | async-start | bytes 1048576 | tf_op jit(solution)/shard_map/psum | solution.py:9
  265.7 420.0 %all-reduce.13.cloned.1.call-start = ((), (), s32[]{:S(2)}) async-start(), calls=%async_computation.1 | async-start | bytes 4194304
  406.9 2.2 copy-start.11
  409.1 1.3 copy-start.10
  410.3 1.3 copy-start.9
  412.9 3.6 copy-start.12
  412.9 273.5 %copy-start.8 = (bf16[4,2,1,8,256]{4,3,2,1,0:T(8,128)(2,1)S(1)}, bf16[4,2,1,8,256]{4,3,2,1,0:T(8,128)(2,1)}, u32[]{:S(2)}) copy-start(bf16[4,2,1,8,256]{4,3,2,1,0:T(8,128)(2,1)} %param.16) | copy-start | bytes 98308
  412.9 277.2 %copy-start.1 = (bf16[6,256,256]{2,1,0:T(8,128)(2,1)S(1)}, bf16[6,256,256]{2,1,0:T(8,128)(2,1)}, u32[]{:S(2)}) copy-start(bf16[6,256,256]{2,1,0:T(8,128)(2,1)} %param.18) | copy-start | bytes 2359300
  412.9 765.9 %all-reduce.11.cloned.1.call-start = ((), (), s32[]{:S(2)}) async-start(), calls=%async_computation | async-start | bytes 5242880 | tf_op jit(solution)/shard_map/psum | solution.py:106
  697.1 481.8 %copy-start.7 = (bf16[4,256,256]{2,1,0:T(8,128)(2,1)S(1)}, bf16[4,256,256]{2,1,0:T(8,128)(2,1)}, u32[]{:S(2)}) copy-start(bf16[4,256,256]{2,1,0:T(8,128)(2,1)} %param.19) | copy-start | bytes 1572868
  1178.9 2.4 copy-start.6
  1179.9 1.7 copy-start.2
  1181.6 1.1 copy-start.5
  1188.4 0.9 copy-start.4
  1194.3 0.9 copy-start.3
Sparse Core Ops, SparseCore 0:
  265.8 140.9 all-reduce.14
  413.1 272.5 all-reduce.12
  697.2 481.5 all-reduce.10
where the time goes:
time: 1210 us
  waiting for transfers between devices  884 us (73%)
  blocking collectives  252 us (21%)
  local copies, waits for them, and re-layouts  20.5 us (2%)
  matrix products  19.6 us (2%)
  other arithmetic  15 us (1%)
  between operations  14.9 us (1%)
    psum x1, waiting for transfers between devices, per_device(): window_sums = lax.psum(jnp.stack(window_parts), ('prow', 'pcol'))  481 us
    unnamed x4, waiting for transfers between devices  262 us
    all_gather x4, blocking collectives, per_device(): full_rows = lax.all_gather(own_piece, 'pcol', axis=1, tiled=True)  252 us
    psum x1, waiting for transfers between devices, broadcast(): return lax.psum(block, axis)  141 us
  transfers between devices with their start and end apart: 3, of which 3 were waited for; matrix products, arithmetic and copies ran while one was open for 1% of the time, Pallas kernels for 0%

commit v1 on v0

--- a/solution.py
+++ b/solution.py
@@ -103,7 +103,7 @@
         factor_rows = own_piece.reshape(tile_rows * slice_rows, width).astype(jnp.float32)
         window_parts = [product(columns[earlier].T, factor_rows) for earlier in range(later)]
         window_parts.append(product(factor_rows.T, current))
-        window_sums = lax.psum(jnp.stack(window_parts), ("prow", "pcol"))
+        window_sums = lax.psum(lax.psum(jnp.stack(window_parts), "prow"), "pcol")
         window_step(later, window_sums, window_factor, diag_inverse, window_blocks)
         columns.append(current)
     ys = jnp.stack(columns).reshape(supernodes, tile_rows, 1, slice_rows, width)

time: 1210 us -> 1150 us (0.950)
  waiting for transfers between devices: 884 us -> 828 us
    psum x1 -> x2, waiting for transfers between devices: 481 us -> 424 us  [per_device(): window_sums = lax.psum(lax.psum(jnp.stack(window_parts), 'prow'), 'pcol')]
    unnamed x4 -> x5, waiting for transfers between devices: 262 us -> 262 us
  transfers between devices with their start and end apart: 3 -> 4, of which waited for: 3 -> 4; matrix products, arithmetic and copies ran while one was open for 1% -> 1% of each run, Pallas kernels for 0% -> 0%
where the time goes in v1:
time: 1150 us
  waiting for transfers between devices  828 us (72%)
  blocking collectives  252 us (22%)
  local copies, waits for them, and re-layouts  20.5 us (2%)
  matrix products  19.6 us (2%)
  other arithmetic  15 us (1%)
  between operations  14.9 us (1%)
    psum x2, waiting for transfers between devices, per_device(): window_sums = lax.psum(lax.psum(jnp.stack(window_parts), 'prow'), 'pcol')  424 us
    unnamed x5, waiting for transfers between devices  262 us
    all_gather x4, blocking collectives, per_device(): full_rows = lax.all_gather(own_piece, 'pcol', axis=1, tiled=True)  252 us
    psum x1, waiting for transfers between devices, broadcast(): return lax.psum(block, axis)  141 us
  transfers between devices with their start and end apart: 4, of which 4 were waited for; matrix products, arithmetic and copies ran while one was open for 1% of the time, Pallas kernels for 0%

profile of v1, /device:TPU:4, one launch (start us, length us, event | category | flops | bytes accessed | tf_op | source)
XLA Modules:
  0.0 1149.5 jit_solution(7416847083691873178)
XLA Ops:
  7.3 0.8 slice_reduce_fusion.1
  8.9 0.8 bitcast_multiply_fusion.6
  9.8 70.2 %all_gather.12 = bf16[2,256,256]{2,0,1:T(2,128)(2,1)S(1)} all-gather(bf16[2,8,256]{2,0,1:T(2,128)(2,1)S(1)} %copy.58), channel_id=1, replica_groups=mesh['prow'=16,'pcol'=32] {'pcol'}, dimensions={1}, use_global_device_ids=true | all-gather | bytes 270336 | tf_op jit(solution)/shard_map/all_gather | solution.py:75
  80.4 59.8 %all_gather.13 = bf16[2,256,256]{2,0,1:T(2,128)(2,1)S(1)} all-gather(bf16[2,8,256]{2,0,1:T(2,128)(2,1)S(1)} %copy.63), channel_id=1, replica_groups=mesh['prow'=16,'pcol'=32] {'pcol'}, dimensions={1}, use_global_device_ids=true | all-gather | bytes 270336 | tf_op jit(solution)/shard_map/all_gather | solution.py:75
  140.7 0.7 select_bitcast_fusion.3
  141.3 0.6 select_bitcast_fusion.2
  142.0 61.7 %all_gather.15 = bf16[2,256,256]{2,0,1:T(2,128)(2,1)S(1)} all-gather(bf16[2,8,256]{2,0,1:T(2,128)(2,1)S(1)} %copy.73), channel_id=1, replica_groups=mesh['prow'=16,'pcol'=32] {'pcol'}, dimensions={1}, use_global_device_ids=true | all-gather | bytes 270336 | tf_op jit(solution)/shard_map/all_gather | solution.py:75
  204.1 0.7 select_bitcast_fusion
  204.8 59.8 %all_gather.14 = bf16[2,256,256]{2,0,1:T(2,128)(2,1)S(1)} all-gather(bf16[2,8,256]{2,0,1:T(2,128)(2,1)S(1)} %copy.68), channel_id=1, replica_groups=mesh['prow'=16,'pcol'=32] {'pcol'}, dimensions={1}, use_global_device_ids=true | all-gather | bytes 270336 | tf_op jit(solution)/shard_map/all_gather | solution.py:75
  265.0 0.7 select_bitcast_fusion.1
  265.8 141.1 %all-reduce.19.cloned.1.call-done = (bf16[256,256]{0,1:T(8,128)(2,1)}, bf16[256,256]{0,1:T(8,128)(2,1)}, bf16[256,256]{0,1:T(8,128)(2,1)}, bf16[256,256]{0,1:T(8,128)(2,1)}) async-done(((bf16[256,256]{0,1:T(8,128)(2,1)}, bf16[256,256]{0,1:T(8,128)(2,1)}, bf16[256,256]{0,1:T(8,128)(2,1)}, bf16[256,256]{0,1:T(8,128)(2,1)}), (bf16[256,256]{0,1:T(8,128)(2,1)}, bf16[256,256]{0,1:T(8,128)(2,1)}, ...) | async-done | bytes 524304 | tf_op jit(solution)/shard_map/psum | solution.py:9
  406.9 1.2 convolution_bitcast_fusion
  408.1 1.0 copy.75
  409.3 1.0 copy.60
  410.6 1.0 copy.65
  411.9 1.0 copy.70
  413.9 0.6 fusion.134
  414.5 0.6 fusion.135
  415.1 0.7 fusion.136
  415.8 0.6 fusion.137
  416.3 5.0 broadcast_select_fusion
  421.4 1.3 dynamic-slice.31
  423.4 262.3 %all-reduce.15.cloned.1.call-done = (f32[256,2,256]{2,1,0:T(2,128)}, f32[256,2,256]{2,1,0:T(2,128)}, f32[256,2,256]{2,1,0:T(2,128)}, f32[256,2,256]{2,1,0:T(2,128)}) async-done(((f32[256,2,256]{2,1,0:T(2,128)}, f32[256,2,256]{2,1,0:T(2,128)}, f32[256,2,256]{2,1,0:T(2,128)}, f32[256,2,256]{2,1,0:T(2,128)}), (f32[256,2,256]{2,1,0:T(2,128)}, f32[256,2,256]{2,1,0:T(2,128)}, f32[256,2,256]{2,1,0:T(2,128)}, ...) | async-done | bytes 2097168
  685.6 0.7 constant_dynamic-slice_fusion.11
  686.3 0.4 convolution_bitcast_fusion.13
  686.7 0.4 convolution_bitcast_fusion.16
  687.1 0.4 convolution_bitcast_fusion.18
  687.5 1.1 convolution_bitcast_fusion.19
  688.6 0.7 constant_dynamic-slice_fusion.10
  689.3 0.7 constant_dynamic-slice_fusion.9
  690.5 0.3 convolution_bitcast_fusion.15
  691.0 0.4 convolution_bitcast_fusion.14
  691.4 0.3 convolution_bitcast_fusion.11
  691.7 0.3 convolution_bitcast_fusion.12
  692.1 0.7 constant_dynamic-slice_fusion.8
  693.2 0.4 convolution_bitcast_fusion.17
  693.8 0.4 convolution_bitcast_fusion.10
  694.2 0.8 pad_maximum_fusion.2
  695.0 0.9 pad_maximum_fusion.1
  695.9 1.1 pad_maximum_fusion
  697.2 147.2 %all-reduce.17.cloned.1.call-done = (f32[1,256,256]{2,1,0:T(8,128)}, f32[4,256,256]{2,1,0:T(8,128)}, f32[2,256,256]{2,1,0:T(8,128)}, f32[3,256,256]{2,1,0:T(8,128)}) async-done(((f32[1,256,256]{2,1,0:T(8,128)}, f32[4,256,256]{2,1,0:T(8,128)}, f32[2,256,256]{2,1,0:T(8,128)}, f32[3,256,256]{2,1,0:T(8,128)}), (f32[1,256,256]{2,1,0:T(8,128)}, f32[4,256,256]{2,1,0:T(8,128)}, f32[2,256,256]{2,1,0:T(8,128)}, ...) | async-done | bytes 2621456 | tf_op jit(solution)/shard_map/psum | solution.py:106
  844.5 0.6 pad_maximum_fusion.3
  845.1 277.1 %all-reduce.13.cloned.1.call-done = (f32[1,256,256]{2,1,0:T(8,128)}, f32[4,256,256]{2,1,0:T(8,128)}, f32[2,256,256]{2,1,0:T(8,128)}, f32[3,256,256]{2,1,0:T(8,128)}) async-done(((f32[1,256,256]{2,1,0:T(8,128)}, f32[4,256,256]{2,1,0:T(8,128)}, f32[2,256,256]{2,1,0:T(8,128)}, f32[3,256,256]{2,1,0:T(8,128)}), (f32[1,256,256]{2,1,0:T(8,128)}, f32[4,256,256]{2,1,0:T(8,128)}, f32[2,256,256]{2,1,0:T(8,128)}, ...) | async-done | bytes 2621456 | tf_op jit(solution)/shard_map/psum | solution.py:106
  1122.3 1.0 subtract_bitcast_fusion
  1123.3 1.3 fusion.14
  1124.6 0.3 fusion.11
  1125.0 0.4 convolution_add_fusion.5
  1125.6 0.4 copy-done.5
  1126.1 0.4 convolution_add_fusion.7
  1127.0 1.0 fusion.7
  1128.1 0.4 convolution_add_fusion.2
  1128.4 0.8 copy.82
  1130.1 0.9 copy.86
  1131.0 0.9 copy.91
  1132.4 0.4 copy-done.4
  1132.8 1.2 fusion.6
  1134.0 0.8 copy.85
  1134.8 2.0 fusion.3
  1136.8 0.8 copy.90
  1137.7 0.4 convolution_add_fusion.1
  1138.0 0.6 copy-done.3
  1139.2 1.9 fusion.1
  1141.3 1.1 maximum_maximum_fusion
  1142.3 0.7 copy.93
  (79 shorter events, 8.7 us)
Async XLA Ops:
  7.2 399.7 %copy-start = (bf16[2,1,256,1,1,256]{5,2,4,3,1,0:T(8,128)(2,1)S(1)}, bf16[2,1,256,1,1,256]{5,2,4,3,1,0:T(8,128)(2,1)}, u32[]{:S(2)}) copy-start(bf16[2,1,256,1,1,256]{5,2,4,3,1,0:T(8,128)(2,1)} %param.15) | copy-start | bytes 786436
  7.2 399.7 %all-reduce.19.cloned.1.call-start = ((), (), s32[]{:S(2)}) async-start(), calls=%async_computation.3 | async-start | bytes 1048576 | tf_op jit(solution)/shard_map/psum | solution.py:9
  265.7 419.9 %all-reduce.15.cloned.1.call-start = ((), (), s32[]{:S(2)}) async-start(), calls=%async_computation.1 | async-start | bytes 4194304
  406.9 2.2 copy-start.11
  409.1 1.3 copy-start.10
  410.3 1.3 copy-start.9
  412.9 3.4 copy-start.12
  412.9 273.4 %copy-start.8 = (bf16[4,2,1,8,256]{4,3,2,1,0:T(8,128)(2,1)S(1)}, bf16[4,2,1,8,256]{4,3,2,1,0:T(8,128)(2,1)}, u32[]{:S(2)}) copy-start(bf16[4,2,1,8,256]{4,3,2,1,0:T(8,128)(2,1)} %param.16) | copy-start | bytes 98308
  412.9 277.1 %copy-start.1 = (bf16[6,256,256]{2,1,0:T(8,128)(2,1)S(1)}, bf16[6,256,256]{2,1,0:T(8,128)(2,1)}, u32[]{:S(2)}) copy-start(bf16[6,256,256]{2,1,0:T(8,128)(2,1)} %param.18) | copy-start | bytes 2359300
  412.9 431.5 %all-reduce.17.cloned.1.call-start = ((), (), s32[]{:S(2)}) async-start(), calls=%async_computation.2 | async-start | bytes 5242880 | tf_op jit(solution)/shard_map/psum | solution.py:106
  697.0 425.2 %all-reduce.13.cloned.1.call-start = ((), (), s32[]{:S(2)}) async-start(), calls=%async_computation | async-start | bytes 5242880 | tf_op jit(solution)/shard_map/psum | solution.py:106
  844.4 277.8 %copy-start.7 = (bf16[4,256,256]{2,1,0:T(8,128)(2,1)S(1)}, bf16[4,256,256]{2,1,0:T(8,128)(2,1)}, u32[]{:S(2)}) copy-start(bf16[4,256,256]{2,1,0:T(8,128)(2,1)} %param.19) | copy-start | bytes 1572868
  1122.2 2.4 copy-start.6
  1123.3 1.7 copy-start.2
  1125.0 1.1 copy-start.5
  1131.8 0.9 copy-start.4
  1137.7 0.9 copy-start.3
Sparse Core Ops, SparseCore 0:
  265.8 140.9 all-reduce.18
  413.1 272.5 all-reduce.14
  697.1 147.2 all-reduce.16
  847.4 274.7 all-reduce.12
